TPU v7x, 32 devices: a whole 2x2x4 slice. The times are simulated.
32 devices in a mesh: pp: 2 (over y), cp: 4 (over z), tp: 4 (over x, core).
Axes of the slice: x: 2, y: 2, z: 4, core: 2. Of those that a mesh axis runs over, the one named last changes fastest.
Arguments:
- query_vectors: bfloat16 [2, 768, 4096], P('pp', 'cp', 'tp'), may hold values from -50 to 50
- key_vectors: bfloat16 [2, 768, 4096], P('pp', 'cp', 'tp'), may hold values from -0.5 to 0.5
- value_vectors: bfloat16 [2, 768, 4096], P('pp', 'cp', 'tp'), may hold values from -150 to 150
- section_inputs: bfloat16 [2, 768, 4096], P('pp', 'cp', 'tp'), may hold values from -6 to 6
- top_grad: bfloat16 [768, 4096], P('cp', 'tp'), may hold values from -6 to 6
- out_gains: float32 [2, 4096], P('pp', 'tp'), may hold values from 0.5 to 2
Outputs:
- section_grads: bfloat16 [2, 768, 4096], P('pp', 'cp', 'tp')
- query_grads: bfloat16 [2, 768, 4096], P('pp', 'cp', 'tp')
- key_grads: bfloat16 [2, 768, 4096], P('pp', 'cp', 'tp')
- value_grads: bfloat16 [2, 768, 4096], P('pp', 'cp', 'tp')
All inputs are finite; a program needn't handle non-finite values.
Results may differ from a plain program's by a relative error of at most 0.01.
Values may be sent and summed in bfloat16 or wider, within the bound.
A program may use at most 64 MiB of HBM per device.

v0:
```python
import functools

import jax
import jax.numpy as jnp
from jax import lax
from jax.experimental import pallas as pl
from jax.experimental.pallas import tpu as pltpu
from jax.sharding import PartitionSpec as P

HEAD = 128
LANES = 128
EPSILON = 1e-06
GROUP = 1
PIECES = 1
VMEM_LIMIT = 24 << 20
MESH = pl.DeviceIdType.MESH
F32 = jnp.float32
BF16 = jnp.bfloat16


def dot(a, b, a_dim, b_dim):
    return lax.dot_general(a, b, (((a_dim,), (b_dim,)), ((), ())), preferred_element_type=F32)


def kernel(
    sizes,
    q_hbm, k_hbm, v_hbm, x_hbm, top_hbm, gain_hbm,
    outs,
    q, k, v, x, top, gain,
    pre_in, pre_out, suf_in, suf_out, states, scores, att, ng, gate, ag, b_out, b_in,
    rows_out, rows_in, inv_out, inv_in,
    in_sem, pre_send, pre_recv, suf_send, suf_recv,
    b_send, b_recv, row_send, row_recv, inv_send, inv_recv,
):
    layers, blocks, shards = sizes
    p = lax.axis_index("pp") if layers > 1 else jnp.int32(0)
    c = lax.axis_index("cp") if blocks > 1 else jnp.int32(0)
    t = lax.axis_index("tp") if shards > 1 else jnp.int32(0)
    rows, width = q.shape
    sec, qg, kg, vg = (outs.at[i] for i in range(4))
    heads = width // HEAD
    groups = [range(h, min(h + GROUP, heads)) for h in range(0, heads, GROUP)]
    padded = rows_out.shape[2]
    total_width = width * shards

    def part(i):
        return slice(i * (HEAD // PIECES), (i + 1) * (HEAD // PIECES))

    def pieces(group):
        return [(h, i) for h in group for i in range(PIECES)]

    def cols(h):
        return slice(h * HEAD, (h + 1) * HEAD)

    loads = [
        pltpu.make_async_copy(k_hbm.at[0], k, in_sem.at[0]),
        pltpu.make_async_copy(v_hbm.at[0], v, in_sem.at[1]),
        pltpu.make_async_copy(q_hbm.at[0], q, in_sem.at[2]),
        pltpu.make_async_copy(x_hbm.at[0], x, in_sem.at[3]),
        pltpu.make_async_copy(gain_hbm, gain, in_sem.at[4]),
        pltpu.make_async_copy(top_hbm, top, in_sem.at[5]),
    ]
    for load in loads[:2]:
        load.start()

    barrier = pltpu.get_barrier_semaphore()

    @pl.when(c > 0)
    def _():
        pl.semaphore_signal(barrier, inc=1, device_id={"cp": c - 1}, device_id_type=MESH)

    @pl.when(c < blocks - 1)
    def _():
        pl.semaphore_signal(barrier, inc=1, device_id={"cp": c + 1}, device_id_type=MESH)

    for d in range(1, shards):
        pl.semaphore_signal(
            barrier, inc=1, device_id={"tp": lax.rem(t + d, shards)}, device_id_type=MESH
        )
    for d in range(1, layers):
        pl.semaphore_signal(
            barrier, inc=1, device_id={"pp": lax.rem(p + d, layers)}, device_id_type=MESH
        )

    @pl.when(c == 0)
    def _():
        pre_in[...] = jnp.zeros_like(pre_in)

    @pl.when(c == blocks - 1)
    def _():
        suf_in[...] = jnp.zeros_like(suf_in)

    for d in range(1, layers):

        @pl.when(p + d >= layers)
        def _():
            b_in[d - 1] = jnp.zeros(b_in.shape[1:], b_in.dtype)
            inv_in[d - 1] = jnp.zeros(inv_in.shape[1:], inv_in.dtype)

    def pre_copy(h, i):
        return pltpu.make_async_remote_copy(
            src_ref=pre_out.at[h, part(i)], dst_ref=pre_in.at[h, part(i)],
            send_sem=pre_send.at[h, i], recv_sem=pre_recv.at[h, i],
            device_id={"cp": c + 1}, device_id_type=MESH,
        )

    def suf_copy(h, i):
        return pltpu.make_async_remote_copy(
            src_ref=suf_out.at[h, part(i)], dst_ref=suf_in.at[h, part(i)],
            send_sem=suf_send.at[h, i], recv_sem=suf_recv.at[h, i],
            device_id={"cp": c - 1}, device_id_type=MESH,
        )

    def b_copy(d, h):
        return pltpu.make_async_remote_copy(
            src_ref=b_out.at[h], dst_ref=b_in.at[d - 1, h],
            send_sem=b_send.at[d - 1, h], recv_sem=b_recv.at[d - 1, h],
            device_id={"pp": p - d}, device_id_type=MESH,
        )

    def inv_copy(d):
        return pltpu.make_async_remote_copy(
            src_ref=inv_out, dst_ref=inv_in.at[d - 1],
            send_sem=inv_send.at[d - 1], recv_sem=inv_recv.at[d - 1],
            device_id={"pp": p - d}, device_id_type=MESH,
        )

    def row_copy(i, d):
        return pltpu.make_async_remote_copy(
            src_ref=rows_out.at[i], dst_ref=rows_in.at[i, d - 1],
            send_sem=row_send.at[i, d - 1], recv_sem=row_recv.at[i, d - 1],
            device_id={"tp": lax.rem(t + d, shards)}, device_id_type=MESH,
        )

    def to_row(partial):
        if padded > rows:
            fill = jnp.zeros((padded - rows, LANES), F32)
            partial = jnp.concatenate([partial, fill], axis=0)
        return jnp.broadcast_to(jnp.sum(partial.T, axis=0, keepdims=True), (8, padded))

    def to_col(row):
        return jnp.broadcast_to(row[0:1], (LANES, padded)).T[:rows]

    def row_start(i, partials):
        ids = lax.broadcasted_iota(jnp.int32, (8, padded), 0)
        packed = to_row(partials[0])
        for j in range(1, len(partials)):
            packed = jnp.where(ids == j, to_row(partials[j]), packed)
        rows_out[i] = packed
        for d in range(1, shards):
            row_copy(i, d).start()

    def row_finish(i):
        total = rows_out[i]
        for d in range(1, shards):
            row_copy(i, d).wait_recv()
            total = total + rows_in[i, d - 1]
        return total

    causal = lax.broadcasted_iota(jnp.int32, (rows, rows), 0) >= lax.broadcasted_iota(
        jnp.int32, (rows, rows), 1
    )

    partners = (shards - 1) + (layers - 1)
    pl.semaphore_wait(
        barrier, partners + jnp.where(c > 0, 1, 0) + jnp.where(c < blocks - 1, 1, 0)
    )

    loads[0].wait()
    loads[1].wait()
    for load in loads[2:]:
        load.start()
    for group in groups:
        for h in group:
            states[h] = dot(k[:, cols(h)], v[:, cols(h)], 0, 0)
        if blocks > 1:

            @pl.when(c == 0)
            def _():
                for h in group:
                    for i in range(PIECES):
                        pre_out[h, part(i)] = states[h, part(i)].astype(BF16)
                        pre_copy(h, i).start()

    for load in loads[2:]:
        load.wait()
    merged = layers <= 2
    squares = jnp.zeros((rows, LANES), F32)
    firsts = jnp.zeros((rows, LANES), F32)
    for group in groups:
        for h in group:
            query, value = q[:, cols(h)], v[:, cols(h)]
            score = jnp.where(causal, dot(query, k[:, cols(h)], 1, 1), 0.0).astype(BF16)
            scores[h] = score
            att[:, cols(h)] = dot(score, value, 1, 0)
            gate[:, cols(h)] = jax.nn.sigmoid(x[:, cols(h)].astype(F32))
        if blocks > 1:

            @pl.when(c > 0)
            def _():
                for h, i in pieces(group):
                    pre_copy(h, i).wait_recv()

                    @pl.when(c < blocks - 1)
                    def _():
                        total = pre_in[h, part(i)].astype(F32) + states[h, part(i)]
                        pre_out[h, part(i)] = total.astype(BF16)
                        pre_copy(h, i).start()

        for h in group:
            attention = att[:, cols(h)] + dot(q[:, cols(h)], pre_in[h], 1, 0)
            att[:, cols(h)] = attention
            squares = squares + attention * attention
            sig = gate[:, cols(h)]
            if merged:
                weighted = top[:, cols(h)].astype(F32) * (gain[:, cols(h)] * sig)
                ng[:, cols(h)] = weighted
                firsts = firsts + weighted * attention
            if layers > 1:
                b_out[h] = (attention * (gain[:, cols(h)] * sig * (1.0 - sig))).astype(BF16)
        for d in range(1, layers):

            @pl.when(p >= d)
            def _():
                for h in group:
                    b_copy(d, h).start()

    row_start(0, (squares, firsts))
    sums = row_finish(0)
    inv_row = 1.0 / jnp.sqrt(sums[0:1] / total_width + EPSILON)
    inv_out[...] = jnp.broadcast_to(inv_row, inv_out.shape)
    for d in range(1, layers):

        @pl.when(p >= d)
        def _():
            inv_copy(d).start()

    inv = to_col(inv_row)

    def wait_inv():
        for d in range(1, layers):

            @pl.when(p + d < layers)
            def _():
                inv_copy(d).wait_recv()

    def wait_b(group):
        for d in range(1, layers):

            @pl.when(p + d < layers)
            def _():
                for h in group:
                    b_copy(d, h).wait_recv()

    def later(h, later_inv):
        incoming = top[:, cols(h)].astype(F32)
        for d in range(1, layers):
            incoming = incoming * (1.0 + b_in[d - 1, h].astype(F32) * later_inv[d - 1])
        return incoming

    if merged:
        mean_row = sums[1:2]
        if layers > 1:
            seconds = jnp.zeros((rows, LANES), F32)
            for group in groups:
                wait_b(group)
                for h in group:
                    seconds = seconds + ng[:, cols(h)] * att[:, cols(h)] * b_in[0, h].astype(F32)

            @pl.when(p < layers - 1)
            def _():
                row_start(1, (seconds,))
                wait_inv()
                total = row_finish(1)
                for d in range(1, shards):
                    row_copy(1, d).wait_send()
                rows_out[1] = total

            @pl.when(p == layers - 1)
            def _():
                rows_out[1] = jnp.zeros(rows_out.shape[1:], F32)

            mean_row = mean_row + inv_in[0, 0:1] * rows_out[1, 0:1]
        mean_row = mean_row * inv_row
        later_inv = [to_col(inv_in[d - 1]) for d in range(1, layers)]
    else:
        wait_inv()
        later_inv = [to_col(inv_in[d - 1]) for d in range(1, layers)]
        products = jnp.zeros((rows, LANES), F32)
        for group in groups:
            wait_b(group)
            for h in group:
                weighted = later(h, later_inv) * (gain[:, cols(h)] * gate[:, cols(h)])
                ng[:, cols(h)] = weighted
                products = products + weighted * att[:, cols(h)] * inv
        row_start(1, (products,))
        mean_row = row_finish(1)
    mean = to_col(mean_row / total_width)
    for group in groups:
        for h in group:
            weighted = ng[:, cols(h)]
            if merged and layers > 1:
                weighted = weighted * (1.0 + b_in[0, h].astype(F32) * later_inv[0])
            grad = ((weighted - att[:, cols(h)] * inv * mean) * inv).astype(BF16)
            ag[:, cols(h)] = grad
            states[h] = dot(q[:, cols(h)], grad, 0, 0)
        if blocks > 1:

            @pl.when(c == blocks - 1)
            def _():
                for h in group:
                    for i in range(PIECES):
                        suf_out[h, part(i)] = states[h, part(i)].astype(BF16)
                        suf_copy(h, i).start()

    for group in groups:
        for h in group:
            sig = gate[:, cols(h)]
            slope = gain[:, cols(h)] * sig * (1.0 - sig)
            factor = 1.0 + att[:, cols(h)] * inv * slope
            sec[:, cols(h)] = (later(h, later_inv) * factor).astype(BF16)
            query, key, value = q[:, cols(h)], k[:, cols(h)], v[:, cols(h)]
            grad = ag[:, cols(h)]
            score_grad = jnp.where(causal, dot(grad, value, 1, 1), 0.0).astype(BF16)
            query_grad = dot(score_grad, key, 1, 0) + dot(grad, pre_in[h], 1, 1)
            qg[:, cols(h)] = query_grad.astype(BF16)
            att[:, cols(h)] = dot(score_grad, query, 0, 0)
            ng[:, cols(h)] = dot(scores[h], grad, 0, 0)
        if blocks > 1:

            @pl.when(c < blocks - 1)
            def _():
                for h, i in pieces(group):
                    suf_copy(h, i).wait_recv()

                    @pl.when(c > 0)
                    def _():
                        total = suf_in[h, part(i)].astype(F32) + states[h, part(i)]
                        suf_out[h, part(i)] = total.astype(BF16)
                        suf_copy(h, i).start()

        for h in group:
            suffix = suf_in[h]
            key_grad = att[:, cols(h)] + dot(v[:, cols(h)], suffix, 1, 1)
            kg[:, cols(h)] = key_grad.astype(BF16)
            value_grad = ng[:, cols(h)] + dot(k[:, cols(h)], suffix, 1, 0)
            vg[:, cols(h)] = value_grad.astype(BF16)

    if blocks > 1:

        @pl.when(c < blocks - 1)
        def _():
            for h, i in pieces(range(heads)):
                pre_copy(h, i).wait_send()

        @pl.when(c > 0)
        def _():
            for h, i in pieces(range(heads)):
                suf_copy(h, i).wait_send()

    for d in range(1, layers):

        @pl.when(p >= d)
        def _():
            inv_copy(d).wait_send()
            for h in range(heads):
                b_copy(d, h).wait_send()

    for d in range(1, shards):
        row_copy(0, d).wait_send()
    if not merged:
        for d in range(1, shards):
            row_copy(1, d).wait_send()


def write_kernel(outs, sec_hbm, qg_hbm, kg_hbm, vg_hbm, sem):
    copies = [
        pltpu.make_async_copy(outs.at[i], dst.at[0], sem.at[i])
        for i, dst in enumerate((sec_hbm, qg_hbm, kg_hbm, vg_hbm))
    ]
    for copy in copies:
        copy.start()
    for copy in copies:
        copy.wait()


def on_device(sizes, q, k, v, x, top, gains):
    layers, blocks, shards = sizes
    rows, width = q.shape[1:]
    heads = width // HEAD
    padded = -(-rows // LANES) * LANES
    others, peers = max(layers - 1, 1), max(shards - 1, 1)
    wide = pltpu.VMEM((rows, width), BF16)
    wide32 = pltpu.VMEM((rows, width), F32)
    square = pltpu.VMEM((heads, HEAD, HEAD), BF16)
    dma = pltpu.SemaphoreType.DMA
    chain = dma((heads, PIECES))
    out = jax.ShapeDtypeStruct((1, rows, width), BF16)
    q, k, v, x, top, gains = (
        pltpu.with_memory_space_constraint(a, pltpu.HBM) for a in (q, k, v, x, top, gains)
    )
    outs = pl.pallas_call(
        functools.partial(kernel, sizes),
        out_shape=jax.ShapeDtypeStruct((4, rows, width), BF16),
        in_specs=[pl.BlockSpec(memory_space=pltpu.HBM)] * 6,
        out_specs=pl.BlockSpec(memory_space=pltpu.VMEM),
        scratch_shapes=[
            wide, wide, wide, wide, wide, pltpu.VMEM((1, width), F32),
            square, square, square, square,
            pltpu.VMEM((heads, HEAD, HEAD), F32),
            pltpu.VMEM((heads, rows, rows), BF16),
            wide32, wide32, wide32, wide,
            pltpu.VMEM((heads, rows, HEAD), BF16),
            pltpu.VMEM((others, heads, rows, HEAD), BF16),
            pltpu.VMEM((2, 8, padded), F32),
            pltpu.VMEM((2, peers, 8, padded), F32),
            pltpu.VMEM((8, padded), F32),
            pltpu.VMEM((others, 8, padded), F32),
            dma((6,)),
            chain, chain, chain, chain,
            dma((others, heads)), dma((others, heads)),
            dma((2, peers)), dma((2, peers)),
            dma((others,)), dma((others,)),
        ],
        compiler_params=pltpu.CompilerParams(collective_id=0, has_side_effects=True, vmem_limit_bytes=VMEM_LIMIT),
    )(q, k, v, x, top, gains)
    return pl.pallas_call(
        write_kernel,
        out_shape=(out,) * 4,
        in_specs=[pl.BlockSpec(memory_space=pltpu.VMEM)],
        out_specs=(pl.BlockSpec(memory_space=pl.ANY),) * 4,
        scratch_shapes=[dma((4,))],
        compiler_params=pltpu.CompilerParams(vmem_limit_bytes=1 << 20),
    )(outs)


def solution(mesh):
    sizes = (mesh.shape["pp"], mesh.shape["cp"], mesh.shape["tp"])
    part = P("pp", "cp", "tp")
    return jax.shard_map(
        functools.partial(on_device, sizes),
        mesh=mesh,
        in_specs=(part, part, part, part, P("cp", "tp"), P("pp", "tp")),
        out_specs=(part, part, part, part),
        check_vma=False,
    )
```

profile of v0, /device:TPU:0, one launch (start us, length us, event | category | flops | bytes accessed | tf_op | source)
XLA Modules:
  0.0 41.2 jit_solution(5003040962653061175)
XLA Ops:
  0.6 39.3 %shard_map.93.outs = bf16[4,192,1024]{2,1,0:T(8,128)(2,1)S(1)} custom-call(bf16[1,192,1024]{2,1,0:T(8,128)(2,1)} %q_hbm.1, bf16[1,192,1024]{2,1,0:T(8,128)(2,1)} %k_hbm.1, bf16[1,192,1024]{2,1,0:T(8,128)(2,1)} %v_hbm.1, bf16[1,192,1024]{2,1,0:T(8,128)(2,1)} %x_hbm.1, bf16[192,1024]{1,0:T(8,128)(2,1)} %top_hbm.1, f32[1,1024]{1,0:T(1,128)} %gain_hbm.1), custom_call_target="tpu_custom_call" | custom-call | tf_op jit(solution)/shard_map/pallas_call | solution.py:402
  40.0 1.2 %shard_map.94 = (bf16[1,192,1024]{2,1,0:T(8,128)(2,1)}, bf16[1,192,1024]{2,1,0:T(8,128)(2,1)}, bf16[1,192,1024]{2,1,0:T(8,128)(2,1)}, bf16[1,192,1024]{2,1,0:T(8,128)(2,1)}) custom-call(bf16[4,192,1024]{2,1,0:T(8,128)(2,1)S(1)} %shard_map.93.outs), custom_call_target="tpu_custom_call" | custom-call | tf_op jit(solution)/shard_map/pallas_call | solution.py:427
where the time goes:
time: 41.3 us; the launch traced here: 41.2 us
  Pallas kernels  40.5 us (98%)
  between operations  0.64 us (2%)
    pallas_call x1, Pallas kernels, on_device(): pl.pallas_call(functools.partial(kernel, sizes), out_shape=jax.ShapeDtype...  39.3 us
    pallas_call x1, Pallas kernels, on_device(): pl.pallas_call(write_kernel, out_shape=(out,) * 4, in_specs=[pl.BlockSpec...  1.17 us

commit v1 on v0

v1 whole, which is shorter than its diff:
```python
import functools

import jax
import jax.numpy as jnp
from jax import lax
from jax.experimental import pallas as pl
from jax.experimental.pallas import tpu as pltpu
from jax.sharding import PartitionSpec as P

HEAD = 128
LANES = 128
EPSILON = 1e-06
PIECES = 4
LEAD = 2
TRAIL = 2
VMEM_LIMIT = 24 << 20
MESH = pl.DeviceIdType.MESH
F32 = jnp.float32
BF16 = jnp.bfloat16


def dot(a, b, a_dim, b_dim):
    return lax.dot_general(a, b, (((a_dim,), (b_dim,)), ((), ())), preferred_element_type=F32)


def kernel(
    sizes,
    q_hbm, k_hbm, v_hbm, x_hbm, top_hbm, gain_hbm,
    outs,
    q, k, v, x, top, gain,
    pre_in, pre_out, suf_in, suf_out, states, scores, att, ng, gate, ag, b_out, b_in,
    rows_out, rows_in, inv_out, inv_in,
    in_sem, chain_send, chain_recv,
    b_send, b_recv, row_send, row_recv, inv_send, inv_recv,
):
    layers, blocks, shards = sizes
    p = lax.axis_index("pp") if layers > 1 else jnp.int32(0)
    c = lax.axis_index("cp") if blocks > 1 else jnp.int32(0)
    t = lax.axis_index("tp") if shards > 1 else jnp.int32(0)
    rows, width = q.shape
    sec, qg, kg, vg = (outs.at[i] for i in range(4))
    heads = width // HEAD
    padded = rows_out.shape[2]
    total_width = width * shards

    def part(i):
        return slice(i * (HEAD // PIECES), (i + 1) * (HEAD // PIECES))

    def cols(h):
        return slice(h * HEAD, (h + 1) * HEAD)

    loads = [
        pltpu.make_async_copy(k_hbm.at[0], k, in_sem.at[0]),
        pltpu.make_async_copy(v_hbm.at[0], v, in_sem.at[1]),
        pltpu.make_async_copy(q_hbm.at[0], q, in_sem.at[2]),
        pltpu.make_async_copy(x_hbm.at[0], x, in_sem.at[3]),
        pltpu.make_async_copy(gain_hbm, gain, in_sem.at[4]),
        pltpu.make_async_copy(top_hbm, top, in_sem.at[5]),
    ]
    for load in loads[:2]:
        load.start()

    barrier = pltpu.get_barrier_semaphore()

    @pl.when(c > 0)
    def _():
        pl.semaphore_signal(barrier, inc=1, device_id={"cp": c - 1}, device_id_type=MESH)

    @pl.when(c < blocks - 1)
    def _():
        pl.semaphore_signal(barrier, inc=1, device_id={"cp": c + 1}, device_id_type=MESH)

    for d in range(1, shards):
        pl.semaphore_signal(
            barrier, inc=1, device_id={"tp": lax.rem(t + d, shards)}, device_id_type=MESH
        )
    for d in range(1, layers):
        pl.semaphore_signal(
            barrier, inc=1, device_id={"pp": lax.rem(p + d, layers)}, device_id_type=MESH
        )

    @pl.when(c == 0)
    def _():
        pre_in[...] = jnp.zeros_like(pre_in)

    @pl.when(c == blocks - 1)
    def _():
        suf_in[...] = jnp.zeros_like(suf_in)

    for d in range(1, layers):

        @pl.when(p + d >= layers)
        def _():
            b_in[d - 1] = jnp.zeros(b_in.shape[1:], b_in.dtype)
            inv_in[d - 1] = jnp.zeros(inv_in.shape[1:], inv_in.dtype)

    def pre_copy(h, i):
        return pltpu.make_async_remote_copy(
            src_ref=pre_out.at[h, part(i)], dst_ref=pre_in.at[h, part(i)],
            send_sem=chain_send.at[0], recv_sem=chain_recv.at[h, i],
            device_id={"cp": c + 1}, device_id_type=MESH,
        )

    def suf_copy(h, i):
        return pltpu.make_async_remote_copy(
            src_ref=suf_out.at[h, part(i)], dst_ref=suf_in.at[h, part(i)],
            send_sem=chain_send.at[1], recv_sem=chain_recv.at[h, i],
            device_id={"cp": c - 1}, device_id_type=MESH,
        )

    def b_copy(d, h):
        return pltpu.make_async_remote_copy(
            src_ref=b_out.at[h], dst_ref=b_in.at[d - 1, h],
            send_sem=b_send.at[d - 1], recv_sem=b_recv.at[d - 1, h],
            device_id={"pp": p - d}, device_id_type=MESH,
        )

    def inv_copy(d):
        return pltpu.make_async_remote_copy(
            src_ref=inv_out, dst_ref=inv_in.at[d - 1],
            send_sem=inv_send.at[d - 1], recv_sem=inv_recv.at[d - 1],
            device_id={"pp": p - d}, device_id_type=MESH,
        )

    def row_copy(i, d):
        return pltpu.make_async_remote_copy(
            src_ref=rows_out.at[i], dst_ref=rows_in.at[i, d - 1],
            send_sem=row_send.at[i], recv_sem=row_recv.at[i],
            device_id={"tp": lax.rem(t + d, shards)}, device_id_type=MESH,
        )

    def to_row(partial):
        if padded > rows:
            fill = jnp.zeros((padded - rows, LANES), F32)
            partial = jnp.concatenate([partial, fill], axis=0)
        return jnp.broadcast_to(jnp.sum(partial.T, axis=0, keepdims=True), (8, padded))

    def to_col(row):
        return jnp.broadcast_to(row[0:1], (LANES, padded)).T[:rows]

    def row_start(i, partials):
        ids = lax.broadcasted_iota(jnp.int32, (8, padded), 0)
        packed = to_row(partials[0])
        for j in range(1, len(partials)):
            packed = jnp.where(ids == j, to_row(partials[j]), packed)
        rows_out[i] = packed
        for d in range(1, shards):
            row_copy(i, d).start()

    def row_all(i):
        return pltpu.make_async_remote_copy(
            src_ref=rows_in.at[i], dst_ref=rows_in.at[i],
            send_sem=row_send.at[i], recv_sem=row_recv.at[i],
            device_id={"tp": lax.rem(t + 1, shards)}, device_id_type=MESH,
        )

    def row_finish(i):
        total = rows_out[i]
        if shards > 1:
            row_all(i).wait_recv()
        for d in range(1, shards):
            total = total + rows_in[i, d - 1]
        return total

    def row_sent(i):
        if shards > 1:
            row_all(i).wait_send()

    causal = lax.broadcasted_iota(jnp.int32, (rows, rows), 0) >= lax.broadcasted_iota(
        jnp.int32, (rows, rows), 1
    )

    def forward(copy, arrived, sent, h, inner, outer):
        @pl.when(inner)
        def _():
            for i in range(PIECES):
                copy(h, i).wait_recv()
                total = arrived[h, part(i)].astype(F32) + states[h, part(i)]
                sent[h, part(i)] = total.astype(BF16)
                copy(h, i).start()

        @pl.when(outer)
        def _():
            for i in range(PIECES):
                copy(h, i).wait_recv()

    def first(copy, sent, h):
        for i in range(PIECES):
            sent[h, part(i)] = states[h, part(i)].astype(BF16)
            copy(h, i).start()

    def local(h):
        query, value = q[:, cols(h)], v[:, cols(h)]
        score = jnp.where(causal, dot(query, k[:, cols(h)], 1, 1), 0.0).astype(BF16)
        scores[h] = score
        att[:, cols(h)] = dot(score, value, 1, 0)
        gate[:, cols(h)] = jax.nn.sigmoid(x[:, cols(h)].astype(F32))

    loads[0].wait()
    loads[1].wait()
    for load in loads[2:]:
        load.start()
    states[0] = dot(k[:, cols(0)], v[:, cols(0)], 0, 0)
    partners = (shards - 1) + (layers - 1)
    pl.semaphore_wait(
        barrier, partners + jnp.where(c > 0, 1, 0) + jnp.where(c < blocks - 1, 1, 0)
    )
    for h in range(heads):
        if h > 0:
            states[h] = dot(k[:, cols(h)], v[:, cols(h)], 0, 0)
        if blocks > 1:

            @pl.when(c == 0)
            def _():
                first(pre_copy, pre_out, h)

    for load in loads[2:]:
        load.wait()
    lead = min(LEAD, heads) if blocks > 1 else heads
    for h in range(lead):
        local(h)
    if lead < heads:

        @pl.when(c != 1)
        def _():
            for h in range(lead, heads):
                local(h)

    merged = layers <= 2
    squares = jnp.zeros((rows, LANES), F32)
    firsts = jnp.zeros((rows, LANES), F32)
    for h in range(heads):
        if blocks > 1:
            forward(pre_copy, pre_in, pre_out, h, (c > 0) & (c < blocks - 1), (c > 0) & (c == blocks - 1))
        attention = att[:, cols(h)] + dot(q[:, cols(h)], pre_in[h], 1, 0)
        att[:, cols(h)] = attention
        squares = squares + attention * attention
        sig = gate[:, cols(h)]
        if merged:
            weighted = top[:, cols(h)].astype(F32) * (gain[:, cols(h)] * sig)
            ng[:, cols(h)] = weighted
            firsts = firsts + weighted * attention
        if layers > 1:
            b_out[h] = (attention * (gain[:, cols(h)] * sig * (1.0 - sig))).astype(BF16)
        for d in range(1, layers):

            @pl.when(p >= d)
            def _():
                b_copy(d, h).start()

        if h + lead < heads:

            @pl.when(c == 1)
            def _():
                local(h + lead)

    row_start(0, (squares, firsts))
    sums = row_finish(0)
    inv_row = 1.0 / jnp.sqrt(sums[0:1] / total_width + EPSILON)
    inv_out[...] = jnp.broadcast_to(inv_row, inv_out.shape)
    for d in range(1, layers):

        @pl.when(p >= d)
        def _():
            inv_copy(d).start()

    inv = to_col(inv_row)

    def wait_inv():
        for d in range(1, layers):

            @pl.when(p + d < layers)
            def _():
                inv_copy(d).wait_recv()

    def wait_b(some):
        for d in range(1, layers):

            @pl.when(p + d < layers)
            def _():
                for h in some:
                    b_copy(d, h).wait_recv()

    def later(h, later_inv):
        incoming = top[:, cols(h)].astype(F32)
        for d in range(1, layers):
            incoming = incoming * (1.0 + b_in[d - 1, h].astype(F32) * later_inv[d - 1])
        return incoming

    if merged:
        mean_row = sums[1:2]
        if layers > 1:
            seconds = jnp.zeros((rows, LANES), F32)
            for h in range(heads):
                wait_b([h])
                seconds = seconds + ng[:, cols(h)] * att[:, cols(h)] * b_in[0, h].astype(F32)

            @pl.when(p < layers - 1)
            def _():
                row_start(1, (seconds,))
                wait_inv()
                total = row_finish(1)
                row_sent(1)
                rows_out[1] = total

            @pl.when(p == layers - 1)
            def _():
                rows_out[1] = jnp.zeros(rows_out.shape[1:], F32)

            mean_row = mean_row + inv_in[0, 0:1] * rows_out[1, 0:1]
        mean_row = mean_row * inv_row
        later_inv = [to_col(inv_in[d - 1]) for d in range(1, layers)]
    else:
        wait_inv()
        later_inv = [to_col(inv_in[d - 1]) for d in range(1, layers)]
        products = jnp.zeros((rows, LANES), F32)
        for h in range(heads):
            wait_b([h])
            weighted = later(h, later_inv) * (gain[:, cols(h)] * gate[:, cols(h)])
            ng[:, cols(h)] = weighted
            products = products + weighted * att[:, cols(h)] * inv
        row_start(1, (products,))
        mean_row = row_finish(1)
    mean = to_col(mean_row / total_width)
    for h in range(heads):
        weighted = ng[:, cols(h)]
        if merged and layers > 1:
            weighted = weighted * (1.0 + b_in[0, h].astype(F32) * later_inv[0])
        grad = ((weighted - att[:, cols(h)] * inv * mean) * inv).astype(BF16)
        ag[:, cols(h)] = grad
        states[h] = dot(q[:, cols(h)], grad, 0, 0)
        if blocks > 1:

            @pl.when(c == blocks - 1)
            def _():
                first(suf_copy, suf_out, h)

    def inner_grads(h):
        sig = gate[:, cols(h)]
        slope = gain[:, cols(h)] * sig * (1.0 - sig)
        factor = 1.0 + att[:, cols(h)] * inv * slope
        sec[:, cols(h)] = (later(h, later_inv) * factor).astype(BF16)
        query, key, value = q[:, cols(h)], k[:, cols(h)], v[:, cols(h)]
        grad = ag[:, cols(h)]
        score_grad = jnp.where(causal, dot(grad, value, 1, 1), 0.0).astype(BF16)
        query_grad = dot(score_grad, key, 1, 0) + dot(grad, pre_in[h], 1, 1)
        qg[:, cols(h)] = query_grad.astype(BF16)
        att[:, cols(h)] = dot(score_grad, query, 0, 0)
        ng[:, cols(h)] = dot(scores[h], grad, 0, 0)

    trail = max(heads - TRAIL, 0) if blocks > 1 else heads
    for h in range(trail):
        inner_grads(h)
    if trail < heads:

        @pl.when(c != blocks - 2)
        def _():
            for h in range(trail, heads):
                inner_grads(h)

    for h in range(heads):
        if blocks > 1:
            forward(suf_copy, suf_in, suf_out, h, (c < blocks - 1) & (c > 0), (c < blocks - 1) & (c == 0))
        if trail + h < heads:

            @pl.when(c == blocks - 2)
            def _():
                inner_grads(trail + h)

        suffix = suf_in[h]
        key_grad = att[:, cols(h)] + dot(v[:, cols(h)], suffix, 1, 1)
        kg[:, cols(h)] = key_grad.astype(BF16)
        value_grad = ng[:, cols(h)] + dot(k[:, cols(h)], suffix, 1, 0)
        vg[:, cols(h)] = value_grad.astype(BF16)

    if blocks > 1:

        @pl.when(c < blocks - 1)
        def _():
            pltpu.make_async_remote_copy(
                src_ref=pre_out, dst_ref=pre_in,
                send_sem=chain_send.at[0], recv_sem=chain_recv.at[0, 0],
                device_id={"cp": c + 1}, device_id_type=MESH,
            ).wait_send()

        @pl.when(c > 0)
        def _():
            pltpu.make_async_remote_copy(
                src_ref=suf_out, dst_ref=suf_in,
                send_sem=chain_send.at[1], recv_sem=chain_recv.at[0, 0],
                device_id={"cp": c - 1}, device_id_type=MESH,
            ).wait_send()

    for d in range(1, layers):

        @pl.when(p >= d)
        def _():
            inv_copy(d).wait_send()
            pltpu.make_async_remote_copy(
                src_ref=b_out, dst_ref=b_in.at[d - 1],
                send_sem=b_send.at[d - 1], recv_sem=b_recv.at[d - 1, 0],
                device_id={"pp": p - d}, device_id_type=MESH,
            ).wait_send()

    row_sent(0)
    if not merged:
        row_sent(1)


def write_kernel(outs, sec_hbm, qg_hbm, kg_hbm, vg_hbm, sem):
    rows = outs.shape[1]
    step = rows // 4 if rows % 32 == 0 else rows
    dsts = (sec_hbm, qg_hbm, kg_hbm, vg_hbm)
    for i, dst in enumerate(dsts):
        for r in range(0, rows, step):
            pltpu.make_async_copy(
                outs.at[i, r : r + step], dst.at[0, r : r + step], sem.at[i]
            ).start()
    for i, dst in enumerate(dsts):
        pltpu.make_async_copy(outs.at[i], dst.at[0], sem.at[i]).wait()


def on_device(sizes, q, k, v, x, top, gains):
    layers, blocks, shards = sizes
    rows, width = q.shape[1:]
    heads = width // HEAD
    padded = -(-rows // LANES) * LANES
    others, peers = max(layers - 1, 1), max(shards - 1, 1)
    wide = pltpu.VMEM((rows, width), BF16)
    wide32 = pltpu.VMEM((rows, width), F32)
    square = pltpu.VMEM((heads, HEAD, HEAD), BF16)
    dma = pltpu.SemaphoreType.DMA
    out = jax.ShapeDtypeStruct((1, rows, width), BF16)
    q, k, v, x, top, gains = (
        pltpu.with_memory_space_constraint(a, pltpu.HBM) for a in (q, k, v, x, top, gains)
    )
    outs = pl.pallas_call(
        functools.partial(kernel, sizes),
        out_shape=jax.ShapeDtypeStruct((4, rows, width), BF16),
        in_specs=[pl.BlockSpec(memory_space=pltpu.HBM)] * 6,
        out_specs=pl.BlockSpec(memory_space=pltpu.VMEM),
        scratch_shapes=[
            wide, wide, wide, wide, wide, pltpu.VMEM((1, width), F32),
            square, square, square, square,
            pltpu.VMEM((heads, HEAD, HEAD), F32),
            pltpu.VMEM((heads, rows, rows), BF16),
            wide32, wide32, wide32, wide,
            pltpu.VMEM((heads, rows, HEAD), BF16),
            pltpu.VMEM((others, heads, rows, HEAD), BF16),
            pltpu.VMEM((2, 8, padded), F32),
            pltpu.VMEM((2, peers, 8, padded), F32),
            pltpu.VMEM((8, padded), F32),
            pltpu.VMEM((others, 8, padded), F32),
            dma((6,)),
            dma((2,)), dma((heads, PIECES)),
            dma((others,)), dma((others, heads)),
            dma((2,)), dma((2,)),
            dma((others,)), dma((others,)),
        ],
        compiler_params=pltpu.CompilerParams(collective_id=0, has_side_effects=True, vmem_limit_bytes=VMEM_LIMIT),
    )(q, k, v, x, top, gains)
    return pl.pallas_call(
        write_kernel,
        out_shape=(out,) * 4,
        in_specs=[pl.BlockSpec(memory_space=pltpu.VMEM)],
        out_specs=(pl.BlockSpec(memory_space=pl.ANY),) * 4,
        scratch_shapes=[dma((4,))],
        compiler_params=pltpu.CompilerParams(vmem_limit_bytes=1 << 20),
    )(outs)


def solution(mesh):
    sizes = (mesh.shape["pp"], mesh.shape["cp"], mesh.shape["tp"])
    part = P("pp", "cp", "tp")
    return jax.shard_map(
        functools.partial(on_device, sizes),
        mesh=mesh,
        in_specs=(part, part, part, part, P("cp", "tp"), P("pp", "tp")),
        out_specs=(part, part, part, part),
        check_vma=False,
    )
```

time: 41.3 us -> 40 us (0.969)
  Pallas kernels: 40.5 us -> 39.2 us
    pallas_call x1, Pallas kernels: 39.3 us -> 38.1 us  [on_device(): pl.pallas_call(functools.partial(kernel, sizes), out_shape=jax.ShapeDtype...]
where the time goes in v1:
time: 40 us; the launch traced here: 39.9 us
  Pallas kernels  39.2 us (98%)
  between operations  0.64 us (2%)
    pallas_call x1, Pallas kernels, on_device(): pl.pallas_call(functools.partial(kernel, sizes), out_shape=jax.ShapeDtype...  38.1 us
    pallas_call x1, Pallas kernels, on_device(): pl.pallas_call(write_kernel, out_shape=(out,) * 4, in_specs=[pl.BlockSpec...  1.16 us

profile of v1, /device:TPU:0, one launch (start us, length us, event | category | flops | bytes accessed | tf_op | source)
XLA Modules:
  0.0 39.9 jit_solution(9865219136176393920)
XLA Ops:
  0.6 38.1 %shard_map.93.outs = bf16[4,192,1024]{2,1,0:T(8,128)(2,1)S(1)} custom-call(bf16[1,192,1024]{2,1,0:T(8,128)(2,1)} %q_hbm.1, bf16[1,192,1024]{2,1,0:T(8,128)(2,1)} %k_hbm.1, bf16[1,192,1024]{2,1,0:T(8,128)(2,1)} %v_hbm.1, bf16[1,192,1024]{2,1,0:T(8,128)(2,1)} %x_hbm.1, bf16[192,1024]{1,0:T(8,128)(2,1)} %top_hbm.1, f32[1,1024]{1,0:T(1,128)} %gain_hbm.1), custom_call_target="tpu_custom_call" | custom-call | tf_op jit(solution)/shard_map/pallas_call | solution.py:437
  38.7 1.2 %shard_map.94 = (bf16[1,192,1024]{2,1,0:T(8,128)(2,1)}, bf16[1,192,1024]{2,1,0:T(8,128)(2,1)}, bf16[1,192,1024]{2,1,0:T(8,128)(2,1)}, bf16[1,192,1024]{2,1,0:T(8,128)(2,1)}) custom-call(bf16[4,192,1024]{2,1,0:T(8,128)(2,1)S(1)} %shard_map.93.outs), custom_call_target="tpu_custom_call" | custom-call | tf_op jit(solution)/shard_map/pallas_call | solution.py:462

commit v2 on v1

--- a/solution.py
+++ b/solution.py
@@ -13,6 +13,7 @@
 PIECES = 4
 LEAD = 2
 TRAIL = 2
+SWAPPED = (3, 5)
 VMEM_LIMIT = 24 << 20
 MESH = pl.DeviceIdType.MESH
 F32 = jnp.float32
@@ -21,6 +22,10 @@
 
 def dot(a, b, a_dim, b_dim):
     return lax.dot_general(a, b, (((a_dim,), (b_dim,)), ((), ())), preferred_element_type=F32)
+
+
+def swapped_heads(heads):
+    return [h for h in SWAPPED if h < heads]
 
 
 def kernel(
@@ -29,9 +34,9 @@
     outs,
     q, k, v, x, top, gain,
     pre_in, pre_out, suf_in, suf_out, states, scores, att, ng, gate, ag, b_out, b_in,
-    rows_out, rows_in, inv_out, inv_in,
+    rows_out, rows_in, inv_out, inv_in, z_out, z_in, mix_out, mix_in,
     in_sem, chain_send, chain_recv,
-    b_send, b_recv, row_send, row_recv, inv_send, inv_recv,
+    b_send, b_recv, row_send, row_recv, inv_send, inv_recv, mix_sem, z_sem,
 ):
     layers, blocks, shards = sizes
     p = lax.axis_index("pp") if layers > 1 else jnp.int32(0)
@@ -41,6 +46,9 @@
     sec, qg, kg, vg = (outs.at[i] for i in range(4))
     heads = width // HEAD
     padded = rows_out.shape[2]
+    swapped = swapped_heads(heads) if layers == 2 else []
+    paired = len(swapped) > 0
+    order = [h for h in range(heads) if h not in swapped] + swapped
     total_width = width * shards
 
     def part(i):
@@ -120,6 +128,34 @@
             src_ref=inv_out, dst_ref=inv_in.at[d - 1],
             send_sem=inv_send.at[d - 1], recv_sem=inv_recv.at[d - 1],
             device_id={"pp": p - d}, device_id_type=MESH,
+        )
+
+    def z_copy(j):
+        return pltpu.make_async_remote_copy(
+            src_ref=z_out.at[j], dst_ref=z_in.at[j],
+            send_sem=z_sem.at[0], recv_sem=z_sem.at[1],
+            device_id={"pp": p + 1}, device_id_type=MESH,
+        )
+
+    def z_all():
+        return pltpu.make_async_remote_copy(
+            src_ref=z_out, dst_ref=z_in,
+            send_sem=z_sem.at[0], recv_sem=z_sem.at[1],
+            device_id={"pp": p + 1}, device_id_type=MESH,
+        )
+
+    def mix_copy(e):
+        return pltpu.make_async_remote_copy(
+            src_ref=mix_out, dst_ref=mix_in.at[e],
+            send_sem=mix_sem.at[0], recv_sem=mix_sem.at[1],
+            device_id={"pp": p - 1, "tp": lax.rem(t + e, shards)}, device_id_type=MESH,
+        )
+
+    def mix_all():
+        return pltpu.make_async_remote_copy(
+            src_ref=mix_in, dst_ref=mix_in,
+            send_sem=mix_sem.at[0], recv_sem=mix_sem.at[1],
+            device_id={"pp": p - 1}, device_id_type=MESH,
         )
 
     def row_copy(i, d):
@@ -226,7 +262,7 @@
             for h in range(lead, heads):
                 local(h)
 
-    merged = layers <= 2
+    merged = layers == 1 or paired
     squares = jnp.zeros((rows, LANES), F32)
     firsts = jnp.zeros((rows, LANES), F32)
     for h in range(heads):
@@ -242,27 +278,56 @@
             firsts = firsts + weighted * attention
         if layers > 1:
             b_out[h] = (attention * (gain[:, cols(h)] * sig * (1.0 - sig))).astype(BF16)
+        if h in swapped:
+
+            @pl.when(p == 0)
+            def _():
+                z_out[swapped.index(h)] = (weighted * attention).astype(BF16)
+                z_copy(swapped.index(h)).start()
+
+        else:
+            for d in range(1, layers):
+
+                @pl.when(p >= d)
+                def _():
+                    b_copy(d, h).start()
+
+        if h + lead < heads:
+
+            @pl.when(c == 1)
+            def _():
+                local(h + lead)
+
+    row_start(0, (squares, firsts))
+    if paired:
+
+        @pl.when(p == 1)
+        def _():
+            seconds = jnp.zeros((rows, LANES), F32)
+            z_all().wait_recv()
+            for j, h in enumerate(swapped):
+                seconds = seconds + z_in[j].astype(F32) * b_out[h].astype(F32)
+            ids = lax.broadcasted_iota(jnp.int32, (8, padded), 0)
+            mix_out[...] = jnp.where(ids == 1, to_row(seconds), rows_out[0])
+            for e in range(shards):
+                mix_copy(e).start()
+
+    sums = row_finish(0)
+    if paired:
+
+        @pl.when(p == 1)
+        def _():
+            for h in swapped:
+                b_copy(1, h).start()
+
+    inv_row = 1.0 / jnp.sqrt(sums[0:1] / total_width + EPSILON)
+    if not paired:
+        inv_out[...] = jnp.broadcast_to(inv_row, inv_out.shape)
         for d in range(1, layers):
 
             @pl.when(p >= d)
             def _():
-                b_copy(d, h).start()
-
-        if h + lead < heads:
-
-            @pl.when(c == 1)
-            def _():
-                local(h + lead)
-
-    row_start(0, (squares, firsts))
-    sums = row_finish(0)
-    inv_row = 1.0 / jnp.sqrt(sums[0:1] / total_width + EPSILON)
-    inv_out[...] = jnp.broadcast_to(inv_row, inv_out.shape)
-    for d in range(1, layers):
-
-        @pl.when(p >= d)
-        def _():
-            inv_copy(d).start()
+                inv_copy(d).start()
 
     inv = to_col(inv_row)
 
@@ -289,27 +354,46 @@
 
     if merged:
         mean_row = sums[1:2]
-        if layers > 1:
-            seconds = jnp.zeros((rows, LANES), F32)
-            for h in range(heads):
-                wait_b([h])
-                seconds = seconds + ng[:, cols(h)] * att[:, cols(h)] * b_in[0, h].astype(F32)
-
-            @pl.when(p < layers - 1)
-            def _():
+        later_inv = []
+        if paired:
+
+            @pl.when(p == 0)
+            def _():
+                seconds = jnp.zeros((rows, LANES), F32)
+                for h in order:
+                    if h not in swapped:
+                        wait_b([h])
+                        seconds = seconds + ng[:, cols(h)] * att[:, cols(h)] * b_in[0, h].astype(F32)
                 row_start(1, (seconds,))
-                wait_inv()
+                mix_all().wait_recv()
+                total = mix_in[0]
+                for e in range(1, shards):
+                    total = total + mix_in[e]
+                above = 1.0 / jnp.sqrt(total[0:1] / total_width + EPSILON)
+                inv_in[0] = jnp.broadcast_to(above, inv_in.shape[1:])
+                inv_out[...] = jnp.broadcast_to(total[1:2], inv_out.shape)
+
+            later_inv = [to_col(inv_in[0])]
+        for h in order:
+            if h not in swapped:
+                scaled = ng[:, cols(h)] * inv
+                if paired:
+                    scaled = scaled * (1.0 + b_in[0, h].astype(F32) * later_inv[0])
+                ng[:, cols(h)] = scaled
+        if paired:
+
+            @pl.when(p == 0)
+            def _():
                 total = row_finish(1)
                 row_sent(1)
-                rows_out[1] = total
-
-            @pl.when(p == layers - 1)
+                rows_out[1] = jnp.broadcast_to(total[0:1] + inv_out[0:1], rows_out.shape[1:])
+
+            @pl.when(p == 1)
             def _():
                 rows_out[1] = jnp.zeros(rows_out.shape[1:], F32)
 
             mean_row = mean_row + inv_in[0, 0:1] * rows_out[1, 0:1]
         mean_row = mean_row * inv_row
-        later_inv = [to_col(inv_in[d - 1]) for d in range(1, layers)]
     else:
         wait_inv()
         later_inv = [to_col(inv_in[d - 1]) for d in range(1, layers)]
@@ -321,12 +405,15 @@
             products = products + weighted * att[:, cols(h)] * inv
         row_start(1, (products,))
         mean_row = row_finish(1)
-    mean = to_col(mean_row / total_width)
-    for h in range(heads):
-        weighted = ng[:, cols(h)]
-        if merged and layers > 1:
-            weighted = weighted * (1.0 + b_in[0, h].astype(F32) * later_inv[0])
-        grad = ((weighted - att[:, cols(h)] * inv * mean) * inv).astype(BF16)
+    scale = to_col(mean_row / total_width * inv_row * inv_row)
+    for h in order:
+        scaled = ng[:, cols(h)]
+        if not merged:
+            scaled = scaled * inv
+        if h in swapped:
+            wait_b([h])
+            scaled = scaled * inv * (1.0 + b_in[0, h].astype(F32) * later_inv[0])
+        grad = (scaled - att[:, cols(h)] * scale).astype(BF16)
         ag[:, cols(h)] = grad
         states[h] = dot(q[:, cols(h)], grad, 0, 0)
         if blocks > 1:
@@ -349,23 +436,23 @@
         ng[:, cols(h)] = dot(scores[h], grad, 0, 0)
 
     trail = max(heads - TRAIL, 0) if blocks > 1 else heads
-    for h in range(trail):
+    for h in order[:trail]:
         inner_grads(h)
     if trail < heads:
 
         @pl.when(c != blocks - 2)
         def _():
-            for h in range(trail, heads):
+            for h in order[trail:]:
                 inner_grads(h)
 
-    for h in range(heads):
+    for place, h in enumerate(order):
         if blocks > 1:
             forward(suf_copy, suf_in, suf_out, h, (c < blocks - 1) & (c > 0), (c < blocks - 1) & (c == 0))
-        if trail + h < heads:
+        if trail + place < heads:
 
             @pl.when(c == blocks - 2)
             def _():
-                inner_grads(trail + h)
+                inner_grads(order[trail + place])
 
         suffix = suf_in[h]
         key_grad = att[:, cols(h)] + dot(v[:, cols(h)], suffix, 1, 1)
@@ -395,12 +482,21 @@
 
         @pl.when(p >= d)
         def _():
-            inv_copy(d).wait_send()
+            if paired:
+                mix_all().wait_send()
+            else:
+                inv_copy(d).wait_send()
             pltpu.make_async_remote_copy(
                 src_ref=b_out, dst_ref=b_in.at[d - 1],
                 send_sem=b_send.at[d - 1], recv_sem=b_recv.at[d - 1, 0],
                 device_id={"pp": p - d}, device_id_type=MESH,
             ).wait_send()
+
+    if swapped:
+
+        @pl.when(p == 0)
+        def _():
+            z_all().wait_send()
 
     row_sent(0)
     if not merged:
@@ -426,6 +522,7 @@
     heads = width // HEAD
     padded = -(-rows // LANES) * LANES
     others, peers = max(layers - 1, 1), max(shards - 1, 1)
+    swaps = max(len(swapped_heads(heads)), 1)
     wide = pltpu.VMEM((rows, width), BF16)
     wide32 = pltpu.VMEM((rows, width), F32)
     square = pltpu.VMEM((heads, HEAD, HEAD), BF16)
@@ -451,11 +548,16 @@
             pltpu.VMEM((2, peers, 8, padded), F32),
             pltpu.VMEM((8, padded), F32),
             pltpu.VMEM((others, 8, padded), F32),
+            pltpu.VMEM((swaps, rows, HEAD), BF16),
+            pltpu.VMEM((swaps, rows, HEAD), BF16),
+            pltpu.VMEM((8, padded), F32),
+            pltpu.VMEM((shards, 8, padded), F32),
             dma((6,)),
             dma((2,)), dma((heads, PIECES)),
             dma((others,)), dma((others, heads)),
             dma((2,)), dma((2,)),
             dma((others,)), dma((others,)),
+            dma((2,)), dma((2,)),
         ],
         compiler_params=pltpu.CompilerParams(collective_id=0, has_side_effects=True, vmem_limit_bytes=VMEM_LIMIT),
     )(q, k, v, x, top, gains)

time: 40 us -> 39.2 us (0.980)
  Pallas kernels: 39.2 us -> 38.4 us
    pallas_call x1, Pallas kernels: 38.1 us -> 37.2 us  [on_device(): pl.pallas_call(functools.partial(kernel, sizes), out_shape=jax.ShapeDtype...]
where the time goes in v2:
time: 39.2 us; the launch traced here: 39 us
  Pallas kernels  38.4 us (98%)
  between operations  0.64 us (2%)
    pallas_call x1, Pallas kernels, on_device(): pl.pallas_call(functools.partial(kernel, sizes), out_shape=jax.ShapeDtype...  37.2 us
    pallas_call x1, Pallas kernels, on_device(): pl.pallas_call(write_kernel, out_shape=(out,) * 4, in_specs=[pl.BlockSpec...  1.16 us

profile of v2, /device:TPU:0, one launch (start us, length us, event | category | flops | bytes accessed | tf_op | source)
XLA Modules:
  0.0 39.0 jit_solution(10941858799536473227)
XLA Ops:
  0.6 37.2 %shard_map.93.outs = bf16[4,192,1024]{2,1,0:T(8,128)(2,1)S(1)} custom-call(bf16[1,192,1024]{2,1,0:T(8,128)(2,1)} %q_hbm.1, bf16[1,192,1024]{2,1,0:T(8,128)(2,1)} %k_hbm.1, bf16[1,192,1024]{2,1,0:T(8,128)(2,1)} %v_hbm.1, bf16[1,192,1024]{2,1,0:T(8,128)(2,1)} %x_hbm.1, bf16[192,1024]{1,0:T(8,128)(2,1)} %top_hbm.1, f32[1,1024]{1,0:T(1,128)} %gain_hbm.1), custom_call_target="tpu_custom_call" | custom-call | tf_op jit(solution)/shard_map/pallas_call | solution.py:534
  37.9 1.2 %shard_map.94 = (bf16[1,192,1024]{2,1,0:T(8,128)(2,1)}, bf16[1,192,1024]{2,1,0:T(8,128)(2,1)}, bf16[1,192,1024]{2,1,0:T(8,128)(2,1)}, bf16[1,192,1024]{2,1,0:T(8,128)(2,1)}) custom-call(bf16[4,192,1024]{2,1,0:T(8,128)(2,1)S(1)} %shard_map.93.outs), custom_call_target="tpu_custom_call" | custom-call | tf_op jit(solution)/shard_map/pallas_call | solution.py:564

commit v3 on v2

--- a/solution.py
+++ b/solution.py
@@ -13,7 +13,8 @@
 PIECES = 4
 LEAD = 2
 TRAIL = 2
-SWAPPED = (3, 5)
+SWAPPED = (3, 5, 6)
+PACKED = 2
 VMEM_LIMIT = 24 << 20
 MESH = pl.DeviceIdType.MESH
 F32 = jnp.float32
@@ -169,13 +170,13 @@
         if padded > rows:
             fill = jnp.zeros((padded - rows, LANES), F32)
             partial = jnp.concatenate([partial, fill], axis=0)
-        return jnp.broadcast_to(jnp.sum(partial.T, axis=0, keepdims=True), (8, padded))
+        return jnp.broadcast_to(jnp.sum(partial.T, axis=0, keepdims=True), (PACKED, padded))
 
     def to_col(row):
         return jnp.broadcast_to(row[0:1], (LANES, padded)).T[:rows]
 
     def row_start(i, partials):
-        ids = lax.broadcasted_iota(jnp.int32, (8, padded), 0)
+        ids = lax.broadcasted_iota(jnp.int32, (PACKED, padded), 0)
         packed = to_row(partials[0])
         for j in range(1, len(partials)):
             packed = jnp.where(ids == j, to_row(partials[j]), packed)
@@ -307,7 +308,7 @@
             z_all().wait_recv()
             for j, h in enumerate(swapped):
                 seconds = seconds + z_in[j].astype(F32) * b_out[h].astype(F32)
-            ids = lax.broadcasted_iota(jnp.int32, (8, padded), 0)
+            ids = lax.broadcasted_iota(jnp.int32, (PACKED, padded), 0)
             mix_out[...] = jnp.where(ids == 1, to_row(seconds), rows_out[0])
             for e in range(shards):
                 mix_copy(e).start()
@@ -544,14 +545,14 @@
             wide32, wide32, wide32, wide,
             pltpu.VMEM((heads, rows, HEAD), BF16),
             pltpu.VMEM((others, heads, rows, HEAD), BF16),
-            pltpu.VMEM((2, 8, padded), F32),
-            pltpu.VMEM((2, peers, 8, padded), F32),
+            pltpu.VMEM((2, PACKED, padded), F32),
+            pltpu.VMEM((2, peers, PACKED, padded), F32),
             pltpu.VMEM((8, padded), F32),
             pltpu.VMEM((others, 8, padded), F32),
             pltpu.VMEM((swaps, rows, HEAD), BF16),
             pltpu.VMEM((swaps, rows, HEAD), BF16),
-            pltpu.VMEM((8, padded), F32),
-            pltpu.VMEM((shards, 8, padded), F32),
+            pltpu.VMEM((PACKED, padded), F32),
+            pltpu.VMEM((shards, PACKED, padded), F32),
             dma((6,)),
             dma((2,)), dma((heads, PIECES)),
             dma((others,)), dma((others, heads)),

time: 39.2 us -> 39 us (level)
  no operation moved by 1% of the time
where the time goes in v3:
time: 39 us; the launch traced here: 38.8 us
  Pallas kernels  38.2 us (98%)
  between operations  0.64 us (2%)
    pallas_call x1, Pallas kernels, on_device(): pl.pallas_call(functools.partial(kernel, sizes), out_shape=jax.ShapeDtype...  37 us
    pallas_call x1, Pallas kernels, on_device(): pl.pallas_call(write_kernel, out_shape=(out,) * 4, in_specs=[pl.BlockSpec...  1.16 us

profile of v3, /device:TPU:0, one launch (start us, length us, event | category | flops | bytes accessed | tf_op | source)
XLA Modules:
  0.0 38.8 jit_solution(1079285972626831073)
XLA Ops:
  0.6 37.0 %shard_map.93.outs = bf16[4,192,1024]{2,1,0:T(8,128)(2,1)S(1)} custom-call(bf16[1,192,1024]{2,1,0:T(8,128)(2,1)} %q_hbm.1, bf16[1,192,1024]{2,1,0:T(8,128)(2,1)} %k_hbm.1, bf16[1,192,1024]{2,1,0:T(8,128)(2,1)} %v_hbm.1, bf16[1,192,1024]{2,1,0:T(8,128)(2,1)} %x_hbm.1, bf16[192,1024]{1,0:T(8,128)(2,1)} %top_hbm.1, f32[1,1024]{1,0:T(1,128)} %gain_hbm.1), custom_call_target="tpu_custom_call" | custom-call | tf_op jit(solution)/shard_map/pallas_call | solution.py:535
  37.7 1.2 %shard_map.94 = (bf16[1,192,1024]{2,1,0:T(8,128)(2,1)}, bf16[1,192,1024]{2,1,0:T(8,128)(2,1)}, bf16[1,192,1024]{2,1,0:T(8,128)(2,1)}, bf16[1,192,1024]{2,1,0:T(8,128)(2,1)}) custom-call(bf16[4,192,1024]{2,1,0:T(8,128)(2,1)S(1)} %shard_map.93.outs), custom_call_target="tpu_custom_call" | custom-call | tf_op jit(solution)/shard_map/pallas_call | solution.py:565

commit v4 on v3

--- a/solution.py
+++ b/solution.py
@@ -12,7 +12,6 @@
 EPSILON = 1e-06
 PIECES = 4
 LEAD = 2
-TRAIL = 2
 SWAPPED = (3, 5, 6)
 PACKED = 2
 VMEM_LIMIT = 24 << 20
@@ -207,7 +206,7 @@
         jnp.int32, (rows, rows), 1
     )
 
-    def forward(copy, arrived, sent, h, inner, outer):
+    def relay(copy, arrived, sent, h, inner):
         @pl.when(inner)
         def _():
             for i in range(PIECES):
@@ -216,6 +215,7 @@
                 sent[h, part(i)] = total.astype(BF16)
                 copy(h, i).start()
 
+    def absorb(copy, h, outer):
         @pl.when(outer)
         def _():
             for i in range(PIECES):
@@ -268,7 +268,8 @@
     firsts = jnp.zeros((rows, LANES), F32)
     for h in range(heads):
         if blocks > 1:
-            forward(pre_copy, pre_in, pre_out, h, (c > 0) & (c < blocks - 1), (c > 0) & (c == blocks - 1))
+            relay(pre_copy, pre_in, pre_out, h, (c > 0) & (c < blocks - 1))
+            absorb(pre_copy, h, (c > 0) & (c == blocks - 1))
         attention = att[:, cols(h)] + dot(q[:, cols(h)], pre_in[h], 1, 0)
         att[:, cols(h)] = attention
         squares = squares + attention * attention
@@ -436,25 +437,14 @@
         att[:, cols(h)] = dot(score_grad, query, 0, 0)
         ng[:, cols(h)] = dot(scores[h], grad, 0, 0)
 
-    trail = max(heads - TRAIL, 0) if blocks > 1 else heads
-    for h in order[:trail]:
+    for h in order:
         inner_grads(h)
-    if trail < heads:
-
-        @pl.when(c != blocks - 2)
-        def _():
-            for h in order[trail:]:
-                inner_grads(h)
-
-    for place, h in enumerate(order):
+    for h in order:
         if blocks > 1:
-            forward(suf_copy, suf_in, suf_out, h, (c < blocks - 1) & (c > 0), (c < blocks - 1) & (c == 0))
-        if trail + place < heads:
-
-            @pl.when(c == blocks - 2)
-            def _():
-                inner_grads(order[trail + place])
-
+            relay(suf_copy, suf_in, suf_out, h, (c < blocks - 1) & (c > 0))
+    for h in order:
+        if blocks > 1:
+            absorb(suf_copy, h, (c < blocks - 1) & (c == 0))
         suffix = suf_in[h]
         key_grad = att[:, cols(h)] + dot(v[:, cols(h)], suffix, 1, 1)
         kg[:, cols(h)] = key_grad.astype(BF16)

time: 39 us -> 38.9 us (level)
  no operation moved by 1% of the time
where the time goes in v4:
time: 38.9 us; the launch traced here: 38.7 us
  Pallas kernels  38.1 us (98%)
  between operations  0.64 us (2%)
    pallas_call x1, Pallas kernels, on_device(): pl.pallas_call(functools.partial(kernel, sizes), out_shape=jax.ShapeDtype...  36.9 us
    pallas_call x1, Pallas kernels, on_device(): pl.pallas_call(write_kernel, out_shape=(out,) * 4, in_specs=[pl.BlockSpec...  1.16 us

profile of v4, /device:TPU:0, one launch (start us, length us, event | category | flops | bytes accessed | tf_op | source)
XLA Modules:
  0.0 38.7 jit_solution(13334206972866380119)
XLA Ops:
  0.6 36.9 %shard_map.93.outs = bf16[4,192,1024]{2,1,0:T(8,128)(2,1)S(1)} custom-call(bf16[1,192,1024]{2,1,0:T(8,128)(2,1)} %q_hbm.1, bf16[1,192,1024]{2,1,0:T(8,128)(2,1)} %k_hbm.1, bf16[1,192,1024]{2,1,0:T(8,128)(2,1)} %v_hbm.1, bf16[1,192,1024]{2,1,0:T(8,128)(2,1)} %x_hbm.1, bf16[192,1024]{1,0:T(8,128)(2,1)} %top_hbm.1, f32[1,1024]{1,0:T(1,128)} %gain_hbm.1), custom_call_target="tpu_custom_call" | custom-call | tf_op jit(solution)/shard_map/pallas_call | solution.py:525
  37.6 1.2 %shard_map.94 = (bf16[1,192,1024]{2,1,0:T(8,128)(2,1)}, bf16[1,192,1024]{2,1,0:T(8,128)(2,1)}, bf16[1,192,1024]{2,1,0:T(8,128)(2,1)}, bf16[1,192,1024]{2,1,0:T(8,128)(2,1)}) custom-call(bf16[4,192,1024]{2,1,0:T(8,128)(2,1)S(1)} %shard_map.93.outs), custom_call_target="tpu_custom_call" | custom-call | tf_op jit(solution)/shard_map/pallas_call | solution.py:555

commit v5 on v4

--- a/solution.py
+++ b/solution.py
@@ -34,7 +34,7 @@
     outs,
     q, k, v, x, top, gain,
     pre_in, pre_out, suf_in, suf_out, states, scores, att, ng, gate, ag, b_out, b_in,
-    rows_out, rows_in, inv_out, inv_in, z_out, z_in, mix_out, mix_in,
+    rows_out, rows_in, inv_out, inv_in, z_out, z_in, mix_out, mix_in, turned,
     in_sem, chain_send, chain_recv,
     b_send, b_recv, row_send, row_recv, inv_send, inv_recv, mix_sem, z_sem,
 ):
@@ -65,9 +65,6 @@
         pltpu.make_async_copy(gain_hbm, gain, in_sem.at[4]),
         pltpu.make_async_copy(top_hbm, top, in_sem.at[5]),
     ]
-    for load in loads[:2]:
-        load.start()
-
     barrier = pltpu.get_barrier_semaphore()
 
     @pl.when(c > 0)
@@ -86,6 +83,9 @@
         pl.semaphore_signal(
             barrier, inc=1, device_id={"pp": lax.rem(p + d, layers)}, device_id_type=MESH
         )
+
+    for load in loads[:2]:
+        load.start()
 
     @pl.when(c == 0)
     def _():
@@ -301,6 +301,8 @@
                 local(h + lead)
 
     row_start(0, (squares, firsts))
+    for h in range(heads):
+        turned[h] = q[:, cols(h)].T
     if paired:
 
         @pl.when(p == 1)
@@ -417,7 +419,7 @@
             scaled = scaled * inv * (1.0 + b_in[0, h].astype(F32) * later_inv[0])
         grad = (scaled - att[:, cols(h)] * scale).astype(BF16)
         ag[:, cols(h)] = grad
-        states[h] = dot(q[:, cols(h)], grad, 0, 0)
+        states[h] = dot(turned[h], grad, 1, 0)
         if blocks > 1:
 
             @pl.when(c == blocks - 1)
@@ -543,6 +545,7 @@
             pltpu.VMEM((swaps, rows, HEAD), BF16),
             pltpu.VMEM((PACKED, padded), F32),
             pltpu.VMEM((shards, PACKED, padded), F32),
+            pltpu.VMEM((heads, HEAD, rows), BF16),
             dma((6,)),
             dma((2,)), dma((heads, PIECES)),
             dma((others,)), dma((others, heads)),

time: 38.9 us -> 38.9 us (level)
  no operation moved by 1% of the time
where the time goes in v5:
time: 38.9 us; the launch traced here: 38.8 us
  Pallas kernels  38.1 us (98%)
  between operations  0.64 us (2%)
    pallas_call x1, Pallas kernels, on_device(): pl.pallas_call(functools.partial(kernel, sizes), out_shape=jax.ShapeDtype...  37 us
    pallas_call x1, Pallas kernels, on_device(): pl.pallas_call(write_kernel, out_shape=(out,) * 4, in_specs=[pl.BlockSpec...  1.16 us

profile of v5, /device:TPU:0, one launch (start us, length us, event | category | flops | bytes accessed | tf_op | source)
XLA Modules:
  0.0 38.8 jit_solution(2812553048259432202)
XLA Ops:
  0.6 37.0 %shard_map.93.outs = bf16[4,192,1024]{2,1,0:T(8,128)(2,1)S(1)} custom-call(bf16[1,192,1024]{2,1,0:T(8,128)(2,1)} %q_hbm.1, bf16[1,192,1024]{2,1,0:T(8,128)(2,1)} %k_hbm.1, bf16[1,192,1024]{2,1,0:T(8,128)(2,1)} %v_hbm.1, bf16[1,192,1024]{2,1,0:T(8,128)(2,1)} %x_hbm.1, bf16[192,1024]{1,0:T(8,128)(2,1)} %top_hbm.1, f32[1,1024]{1,0:T(1,128)} %gain_hbm.1), custom_call_target="tpu_custom_call" | custom-call | tf_op jit(solution)/shard_map/pallas_call | solution.py:527
  37.6 1.2 %shard_map.94 = (bf16[1,192,1024]{2,1,0:T(8,128)(2,1)}, bf16[1,192,1024]{2,1,0:T(8,128)(2,1)}, bf16[1,192,1024]{2,1,0:T(8,128)(2,1)}, bf16[1,192,1024]{2,1,0:T(8,128)(2,1)}) custom-call(bf16[4,192,1024]{2,1,0:T(8,128)(2,1)S(1)} %shard_map.93.outs), custom_call_target="tpu_custom_call" | custom-call | tf_op jit(solution)/shard_map/pallas_call | solution.py:558
